TPU v7x, 128 devices: a whole 4x4x4 slice. The times are simulated.
128 devices in a mesh: dp: 64 (over y, x_lo, z, core), tensor: 2 (over x_hi).
Axes of the slice: x: 4 (x_hi: 2, x_lo: 2; x = x_hi * 2 + x_lo), y: 4, z: 4, core: 2. Of those that a mesh axis runs over, the one named last changes fastest.
Arguments:
- tokens: bfloat16 [64, 512, 896], P(None, 'dp'), may hold values from -6 to 6
- cotangent: bfloat16 [64, 512, 896], P(None, 'dp'), may hold values from -6 to 6
- lengths: int32 [64], replicated, may hold values from 1 to 512, 24576 in all
- deal_order: int32 [64], replicated, may hold values from 0 to 63, each once
- gain_attn: bfloat16 [896], replicated, may hold values from 0.099609375 to 1.8984375
- w_query: bfloat16 [896, 896], P(None, 'tensor'), may hold values from -0.1875 to 0.1875
- b_query: bfloat16 [896], P('tensor'), may hold values from -3 to 3
- w_key: bfloat16 [896, 128], P(None, 'tensor'), may hold values from -0.1875 to 0.1875
- b_key: bfloat16 [128], P('tensor'), may hold values from -3 to 3
- w_value: bfloat16 [896, 128], P(None, 'tensor'), may hold values from -0.1875 to 0.1875
- b_value: bfloat16 [128], P('tensor'), may hold values from -3 to 3
- w_out: bfloat16 [896, 896], P('tensor'), may hold values from -1 to 1
- gain_mlp: bfloat16 [896], replicated, may hold values from 0.099609375 to 1.8984375
- w_gate: bfloat16 [896, 4864], P(None, 'tensor'), may hold values from -0.1875 to 0.1875
- w_up: bfloat16 [896, 4864], P(None, 'tensor'), may hold values from -0.1875 to 0.1875
- w_down: bfloat16 [4864, 896], P('tensor'), may hold values from -0.078125 to 0.078125
Outputs:
- layer_out: bfloat16 [64, 512, 896], P(None, 'dp')
- grad_tokens: bfloat16 [64, 512, 896], P(None, 'dp')
- grad_gain_attn: float32 [896], replicated
- grad_w_query: float32 [896, 896], P(None, 'tensor')
- grad_b_query: float32 [896], P('tensor')
- grad_w_key: float32 [896, 128], P(None, 'tensor')
- grad_b_key: float32 [128], P('tensor')
- grad_w_value: float32 [896, 128], P(None, 'tensor')
- grad_b_value: float32 [128], P('tensor')
- grad_w_out: float32 [896, 896], P('tensor')
- grad_gain_mlp: float32 [896], replicated
- grad_w_gate: float32 [896, 4864], P(None, 'tensor')
- grad_w_up: float32 [896, 4864], P(None, 'tensor')
- grad_w_down: float32 [4864, 896], P('tensor')
- rms_values: float32 [3], replicated
Inputs may be any that keep to these rules, and one draw needn't show every extreme that they name: Group g receives stored slot deal_order[g]; every slot goes to exactly one group. The first lengths[g] rows of the slot that group g receives are valid.
All inputs are finite; a program needn't handle non-finite values.
Results may differ from a plain program's by a relative error of at most 0.022.
Values may be sent and summed in bfloat16 or wider, within the bound.
A program may use at most 192 MiB of HBM per device.

v0:
```python
import math
import jax
import jax.numpy as jnp
from jax import lax
from jax.sharding import PartitionSpec as P

HD = 64
epsilon = 1e-06
rope_base = 1000000.0


def rope_tables(seq_rows, head_size):
    places = jnp.arange(seq_rows).astype(jnp.float32)
    frequency = rope_base ** (-jnp.arange(head_size // 2).astype(jnp.float32) * 2.0 / head_size)
    angles = places[:, None] * frequency[None, :]
    return (jnp.cos(angles)[:, None, :], jnp.sin(angles)[:, None, :])


def rotate(tensor, cos_table, sine_table):
    half_width = tensor.shape[-1] // 2
    first_half = tensor[..., :half_width]
    second_half = tensor[..., half_width:]
    return jnp.concatenate(
        [
            first_half * cos_table - second_half * sine_table,
            second_half * cos_table + first_half * sine_table,
        ],
        axis=-1,
    )


def unrotate(grad_rot, cos_table, sine_table):
    half_width = grad_rot.shape[-1] // 2
    first_half = grad_rot[..., :half_width]
    second_half = grad_rot[..., half_width:]
    return jnp.concatenate(
        [
            first_half * cos_table + second_half * sine_table,
            second_half * cos_table - first_half * sine_table,
        ],
        axis=-1,
    )


def dot_left(matrix, other):
    return lax.dot_general(
        matrix, other, (((0,), (0,)), ((), ())), preferred_element_type=jnp.float32
    )


def dot_right(matrix, other):
    return lax.dot_general(
        matrix, other, (((1,), (1,)), ((), ())), preferred_element_type=jnp.float32
    )


def on_device(
    tokens,
    cotangent,
    lengths,
    deal_order,
    gain_attn,
    w_query,
    b_query,
    w_key,
    b_key,
    w_value,
    b_value,
    w_out,
    gain_mlp,
    w_gate,
    w_up,
    w_down,
):
    restore = jnp.argsort(deal_order)
    arrived = (
        lax.all_to_all(tokens[deal_order], "dp", split_axis=0, concat_axis=1, tiled=True),
        lax.all_to_all(cotangent[deal_order], "dp", split_axis=0, concat_axis=1, tiled=True),
    )
    stream = arrived[0][0].astype(jnp.float32)
    grad_out = arrived[1][0].astype(jnp.float32)
    seq_rows, width = stream.shape
    head_size = HD
    length = lengths[lax.axis_index("dp")]
    places = jnp.arange(seq_rows)
    usable = places < length
    row_mask = usable[:, None]
    cos_table, sine_table = rope_tables(seq_rows, head_size)
    local_heads = w_query.shape[1] // head_size
    local_kv = w_key.shape[1] // head_size
    group_size = local_heads // local_kv
    score_scale = 1.0 / math.sqrt(head_size)
    allowed = (places[None, :] <= places[:, None]) & usable[None, :]
    gain_one = gain_attn.astype(jnp.float32)
    gain_two = gain_mlp.astype(jnp.float32)
    inverse_one = lax.rsqrt(jnp.mean(stream * stream, axis=-1, keepdims=True) + epsilon)
    normed = (stream * inverse_one * gain_one).astype(jnp.bfloat16)
    q_lin = jnp.dot(normed, w_query, preferred_element_type=jnp.float32) + b_query.astype(
        jnp.float32
    )
    k_lin = jnp.dot(normed, w_key, preferred_element_type=jnp.float32) + b_key.astype(jnp.float32)
    v_lin = jnp.dot(normed, w_value, preferred_element_type=jnp.float32) + b_value.astype(
        jnp.float32
    )
    queries = rotate(q_lin.reshape(seq_rows, local_heads, head_size), cos_table, sine_table).astype(
        jnp.bfloat16
    )
    queries = queries.reshape(seq_rows, local_kv, group_size, head_size)
    keys_rot = rotate(k_lin.reshape(seq_rows, local_kv, head_size), cos_table, sine_table).astype(
        jnp.bfloat16
    )
    values = v_lin.reshape(seq_rows, local_kv, head_size).astype(jnp.bfloat16)
    raw_scores = jnp.einsum("qkgd,pkd->kgqp", queries, keys_rot, preferred_element_type=jnp.float32)
    scores = jnp.where(allowed, raw_scores * score_scale, -1e30)
    top_score = jnp.max(scores, axis=-1, keepdims=True)
    expo = jnp.exp(scores - top_score)
    total = jnp.sum(expo, axis=-1, keepdims=True)
    log_total = top_score + jnp.log(total)
    probs_low = (expo / total).astype(jnp.bfloat16)
    mixed = jnp.einsum("kgqp,pkd->qkgd", probs_low, values, preferred_element_type=jnp.float32)
    mixed = mixed.reshape(seq_rows, local_heads * head_size).astype(jnp.bfloat16)
    attention = lax.psum(jnp.dot(mixed, w_out, preferred_element_type=jnp.float32), "tensor")
    residual = stream + attention
    inverse_two = lax.rsqrt(jnp.mean(residual * residual, axis=-1, keepdims=True) + epsilon)
    normed_two = (residual * inverse_two * gain_two).astype(jnp.bfloat16)
    gate_lin = jnp.dot(normed_two, w_gate, preferred_element_type=jnp.float32)
    up_lin = jnp.dot(normed_two, w_up, preferred_element_type=jnp.float32)
    sigmoid_gate = jax.nn.sigmoid(gate_lin)
    silu_gate = gate_lin * sigmoid_gate
    hidden = (silu_gate * up_lin).astype(jnp.bfloat16)
    mlp_branch = lax.psum(
        jnp.dot(hidden, w_down, preferred_element_type=jnp.float32).astype(jnp.bfloat16), "tensor"
    ).astype(jnp.float32)
    result = jnp.where(row_mask, residual + mlp_branch, 0.0)
    statistics = jnp.stack(
        [
            jnp.sum(result * result),
            jnp.sum(jnp.where(row_mask, attention * attention, 0.0)),
            jnp.sum(jnp.where(row_mask, mlp_branch * mlp_branch, 0.0)),
        ]
    )
    grad_y = jnp.where(row_mask, grad_out, 0.0)
    grad_low = grad_y.astype(jnp.bfloat16)
    grad_w_down = dot_left(hidden, grad_low)
    grad_hidden = dot_right(grad_low, w_down)
    grad_gate = (
        grad_hidden * up_lin * sigmoid_gate * (1.0 + gate_lin * (1.0 - sigmoid_gate))
    ).astype(jnp.bfloat16)
    grad_up = (grad_hidden * silu_gate).astype(jnp.bfloat16)
    grad_w_gate = dot_left(normed_two, grad_gate)
    grad_w_up = dot_left(normed_two, grad_up)
    grad_normed_two = lax.psum(dot_right(grad_gate, w_gate) + dot_right(grad_up, w_up), "tensor")
    grad_gain_mlp = jnp.sum(grad_normed_two * residual * inverse_two, axis=0)
    scaled_two = grad_normed_two * gain_two
    grad_resid = (
        grad_y
        + inverse_two * scaled_two
        - residual * inverse_two**3 * jnp.mean(scaled_two * residual, axis=-1, keepdims=True)
    )
    grad_attn = grad_resid.astype(jnp.bfloat16)
    grad_w_out = dot_left(mixed, grad_attn)
    grad_mixed = dot_right(grad_attn, w_out).astype(jnp.bfloat16)
    grad_mixed = grad_mixed.reshape(seq_rows, local_kv, group_size, head_size)
    probs = jnp.exp(scores - log_total)
    grad_probs = jnp.einsum(
        "qkgd,pkd->kgqp", grad_mixed, values, preferred_element_type=jnp.float32
    )
    grad_values = jnp.einsum(
        "kgqp,qkgd->pkd", probs_low, grad_mixed, preferred_element_type=jnp.float32
    )
    row_inner = jnp.sum(probs * grad_probs, axis=-1, keepdims=True)
    grad_scores = (probs * (grad_probs - row_inner) * score_scale).astype(jnp.bfloat16)
    grad_queries = jnp.einsum(
        "kgqp,pkd->qkgd", grad_scores, keys_rot, preferred_element_type=jnp.float32
    )
    grad_keys = jnp.einsum(
        "kgqp,qkgd->pkd", grad_scores, queries, preferred_element_type=jnp.float32
    )
    grad_q_lin = unrotate(
        grad_queries.reshape(seq_rows, local_heads, head_size), cos_table, sine_table
    )
    grad_q_lin = grad_q_lin.reshape(seq_rows, local_heads * head_size).astype(jnp.bfloat16)
    grad_k_lin = (
        unrotate(grad_keys, cos_table, sine_table)
        .reshape(seq_rows, local_kv * head_size)
        .astype(jnp.bfloat16)
    )
    grad_v_lin = grad_values.reshape(seq_rows, local_kv * head_size).astype(jnp.bfloat16)
    grad_w_query = dot_left(normed, grad_q_lin)
    grad_w_key = dot_left(normed, grad_k_lin)
    grad_w_value = dot_left(normed, grad_v_lin)
    grad_b_query = jnp.sum(grad_q_lin.astype(jnp.float32), axis=0)
    grad_b_key = jnp.sum(grad_k_lin.astype(jnp.float32), axis=0)
    grad_b_value = jnp.sum(grad_v_lin.astype(jnp.float32), axis=0)
    grad_normed = lax.psum(
        (
            dot_right(grad_q_lin, w_query)
            + dot_right(grad_k_lin, w_key)
            + dot_right(grad_v_lin, w_value)
        ).astype(jnp.bfloat16),
        "tensor",
    ).astype(jnp.float32)
    grad_gain_attn = jnp.sum(grad_normed * stream * inverse_one, axis=0)
    scaled_one = grad_normed * gain_one
    grad_stream = (
        grad_resid
        + inverse_one * scaled_one
        - stream * inverse_one**3 * jnp.mean(scaled_one * stream, axis=-1, keepdims=True)
    )
    (
        statistics,
        grad_gain_attn,
        grad_w_query,
        grad_b_query,
        grad_w_key,
        grad_b_key,
        grad_w_value,
        grad_b_value,
        grad_w_out,
        grad_gain_mlp,
        grad_w_gate,
        grad_w_up,
        grad_w_down,
    ) = lax.psum(
        (
            statistics,
            grad_gain_attn,
            grad_w_query,
            grad_b_query,
            grad_w_key,
            grad_b_key,
            grad_w_value,
            grad_b_value,
            grad_w_out,
            grad_gain_mlp,
            grad_w_gate,
            grad_w_up,
            grad_w_down,
        ),
        "dp",
    )
    sent_back = (
        lax.all_to_all(
            result.astype(jnp.bfloat16)[None], "dp", split_axis=1, concat_axis=0, tiled=True
        ),
        lax.all_to_all(
            grad_stream.astype(jnp.bfloat16)[None], "dp", split_axis=1, concat_axis=0, tiled=True
        ),
    )
    layer_out = sent_back[0][restore]
    grad_tokens = sent_back[1][restore]
    count = jnp.sum(lengths).astype(jnp.float32) * width
    rms_values = jnp.sqrt(statistics / count)
    return (
        layer_out,
        grad_tokens,
        grad_gain_attn,
        grad_w_query,
        grad_b_query,
        grad_w_key,
        grad_b_key,
        grad_w_value,
        grad_b_value,
        grad_w_out,
        grad_gain_mlp,
        grad_w_gate,
        grad_w_up,
        grad_w_down,
        rms_values,
    )


def solution(mesh):
    in_specs = (
        P(None, "dp", None),
        P(None, "dp", None),
        P(),
        P(),
        P(),
        P(None, "tensor"),
        P("tensor"),
        P(None, "tensor"),
        P("tensor"),
        P(None, "tensor"),
        P("tensor"),
        P("tensor", None),
        P(),
        P(None, "tensor"),
        P(None, "tensor"),
        P("tensor", None),
    )
    out_specs = (
        P(None, "dp", None),
        P(None, "dp", None),
        P(),
        P(None, "tensor"),
        P("tensor"),
        P(None, "tensor"),
        P("tensor"),
        P(None, "tensor"),
        P("tensor"),
        P("tensor", None),
        P(),
        P(None, "tensor"),
        P(None, "tensor"),
        P("tensor", None),
        P(),
    )
    return jax.shard_map(
        on_device, mesh=mesh, in_specs=in_specs, out_specs=out_specs, check_vma=False
    )
```

profile of v0, /device:TPU:0, one launch (start us, length us, event | category | flops | bytes accessed | tf_op | source)
XLA Modules:
  0.0 1022.6 jit_solution(5831000406995036942)
XLA Ops:
  8.4 1.6 gather_fusion
  10.0 10.1 all-to-all-start
  22.0 14.5 %all-to-all-done = bf16[64,8,896]{2,1,0:T(8,128)(2,1)S(1)} async-done(((bf16[64,8,896]{2,1,0:T(8,128)(2,1)}), bf16[64,8,896]{2,1,0:T(8,128)(2,1)S(1)}, u32[]{:S(2)}, u32[]{:S(2)}) %all-to-all-start) | async-done | bytes 917536 | tf_op jit(solution)/shard_map/all_to_all | solution.py:77
  37.7 0.8 convolution_add_fusion.1
  38.7 1.3 fusion.6
  40.0 1.5 fusion.4
  42.1 0.8 copy-done.2
  42.9 2.3 fusion.36
  45.2 0.7 copy-done.8
  46.0 2.0 fusion.103
  48.0 1.6 gather_fusion.2
  49.6 5.5 all-to-all-start.2
  55.3 65.8 %all-reduce.8.cloned.1.call-done = f32[512,896]{1,0:T(8,128)} async-done(((f32[512,896]{1,0:T(8,128)}), f32[512,896]{1,0:T(8,128)}) %all-reduce.8.cloned.1.call-update) | async-done | bytes 1835024 | tf_op jit(solution)/shard_map/psum | solution.py:122
  121.1 1.8 multiply_reduce_fusion.3
  124.5 7.2 fusion.104
  131.7 4.5 fusion.105
  136.2 10.4 %multiply_convert_fusion = (bf16[512,2432]{1,0:T(8,128)(2,1)}, bf16[512,2432]{1,0:T(8,128)(2,1)}, bf16[512,2432]{1,0:T(8,128)(2,1)S(1)}) fusion(f32[512,2432]{1,0:T(8,128)} %fusion.104, f32[512,2432]{1,0:T(8,128)} %fusion.105, bf16[2432,896]{1,0:T(8,128)(2,1)} %param.31, bf16[64,8,896]{2,1,0:T(8,128)(2,1)} %all-to-all-done.2, ...), kind=kOutput, calls=%fused_computation.15 | convolution fusion | flops 2251423744 | bytes 22708736 | tf_op jit(solution)/shard_map/dot_general | solution.py:52
  146.6 1.5 copy-done.61
  148.0 6.0 convolution_convert_fusion
  154.1 6.0 fusion.106
  160.1 6.4 convolution_add_fusion
  167.7 8.2 fusion.108
  176.0 6.1 fusion.109
  182.1 7.5 fusion.65
  189.6 9.3 all-reduce.10.cloned.1.call-done
  198.9 67.2 %all-reduce.12.cloned.1.call-done = f32[512,896]{1,0:T(8,128)} async-done(((f32[512,896]{1,0:T(8,128)}), f32[512,896]{1,0:T(8,128)}) %all-reduce.12.cloned.1.call-update) | async-done | bytes 1835024 | tf_op jit(solution)/shard_map/psum | solution.py:152
  266.2 5.5 select_reduce_fusion
  271.8 2.5 fusion.35
  275.2 2.4 fusion
  277.6 2.4 fusion.7
  280.0 0.7 convolution_bitcast_fusion
  280.8 1.2 convolution_bitcast_fusion.1
  282.1 2.3 convert_reduce_fusion.1
  284.7 0.8 copy-done.15
  287.0 1.4 add_convert_fusion
  288.7 1.1 fusion.61
  289.8 1.1 fusion.63
  291.0 1.9 fusion.59
  292.9 1.8 fusion.56
  294.7 3.8 copy.64
  299.1 8.1 reduce.8
  307.2 2.9 reshape.436
  310.1 8.4 all-to-all-start.1
  318.5 22.4 %all-reduce.14.cloned.1.call-done = bf16[512,896]{1,0:T(8,128)(2,1)} async-done(((bf16[512,896]{1,0:T(8,128)(2,1)}), bf16[512,896]{1,0:T(8,128)(2,1)}) %all-reduce.14.cloned.1.call-update) | async-done | bytes 917520 | tf_op jit(solution)/shard_map/psum | solution.py:195
  340.9 2.0 fusion.29
  343.0 1.7 fusion.55
  344.7 1.4 copy.63
  346.1 6.2 reduce.9
  352.4 1.3 reshape.438
  353.7 8.3 all-to-all-start.3
  362.7 2.0 sort.17
  365.6 2.1 pad_maximum_fusion.3
  367.6 5.4 reshape.437
  373.0 1.0 copy.62
  374.1 2.8 gather_fusion.1
  376.8 280.9 %all-reduce = (f32[896]{0:T(1024)}, f32[448]{0:T(512)}, f32[64]{0:T(128)}, f32[64]{0:T(128)}, f32[896]{0:T(1024)}, /*index=5*/f32[3]{0:T(128)S(1)}) all-reduce(f32[896]{0:T(1024)S(1)} %get-tuple-element.20, f32[448]{0:T(512)S(1)} %reduce_sum.145, f32[64]{0:T(128)S(1)} %convert_reduce_fusion.2, ...), channel_id=1, replica_groups=mesh['dp'=64,'tensor'=2] {'dp'}, use_global_device_ids=true, to_apply=%region_13.14 | all-reduce | flops 2371 | bytes 18968 | tf_op jit(solution)/shard_map/psum | solution.py:224
  659.1 1.6 gather_fusion.3
  660.7 331.3 %all-reduce.16.cloned.1.call-done = (f32[896,448]{0,1:T(8,128)}, f32[896,64]{0,1:T(8,128)}, f32[896,64]{0,1:T(8,128)}, f32[448,896]{1,0:T(8,128)}, f32[896,2432]...) async-done(((f32[896,448]{0,1:T(8,128)}, f32[896,64]{0,1:T(8,128)}, f32[896,64]{0,1:T(8,128)}, f32[448,896]{1,0:T(8,128)}, f32[896,2432]{1,0:T(8,128)}, ...) | async-done | bytes 29818896 | tf_op jit(solution)/shard_map/psum | solution.py:224
  992.0 2.8 copy.76
  996.2 1.2 copy.79
  997.4 8.6 copy.80
  1006.0 4.4 copy.81
  1010.4 1.6 slice-done.3
  1012.1 3.5 copy.82
  (199 shorter events, 15.1 us)
Async XLA Ops:
  7.2 12.9 %copy-start.56 = (bf16[64]{0:T(256)(128)(2,1)S(1)}, bf16[64]{0:T(256)(128)(2,1)}, u32[]{:S(2)}) copy-start(bf16[64]{0:T(256)(128)(2,1)} %param.26) | copy-start | bytes 388
  7.2 12.9 %copy-start.53 = (bf16[896]{0:T(1024)(128)(2,1)S(1)}, bf16[896]{0:T(1024)(128)(2,1)}, u32[]{:S(2)}) copy-start(bf16[896]{0:T(1024)(128)(2,1)} %param.20) | copy-start | bytes 5380
  7.2 13.0 %copy-start.55 = (bf16[448]{0:T(512)(128)(2,1)S(1)}, bf16[448]{0:T(512)(128)(2,1)}, u32[]{:S(2)}) copy-start(bf16[448]{0:T(512)(128)(2,1)} %param.22) | copy-start | bytes 2692
  7.2 13.0 %copy-start.57 = (bf16[64]{0:T(256)(128)(2,1)S(1)}, bf16[64]{0:T(256)(128)(2,1)}, u32[]{:S(2)}) copy-start(bf16[64]{0:T(256)(128)(2,1)} %param.24) | copy-start | bytes 388
  7.2 13.0 %copy-start.58 = (s32[64]{0:T(128)S(1)}, s32[64]{0:T(128)}, u32[]{:S(2)}) copy-start(s32[64]{0:T(128)} %param.18) | copy-start | bytes 772
  8.4 28.5 %copy-start.26 = (bf16[896,64]{0,1:T(8,128)(2,1)S(1)}, bf16[896,64]{0,1:T(8,128)(2,1)}, u32[]{:S(2)}) copy-start(bf16[896,64]{0,1:T(8,128)(2,1)} %param.23) | copy-start | bytes 344068
  10.0 27.7 %copy-start.14 = (bf16[896,448]{0,1:T(8,128)(2,1)S(1)}, bf16[896,448]{0,1:T(8,128)(2,1)}, u32[]{:S(2)}) copy-start(bf16[896,448]{0,1:T(8,128)(2,1)} %param.21) | copy-start | bytes 2408452
  10.0 26.5 %all-to-all-start = ((bf16[64,8,896]{2,1,0:T(8,128)(2,1)}), bf16[64,8,896]{2,1,0:T(8,128)(2,1)S(1)}, u32[]{:S(2)}, u32[]{:S(2)}) async-start(bf16[64,8,896]{2,1,0:T(8,128)(2,1)} %gather_fusion), calls=%async_computation | async-start | bytes 1835008 | tf_op jit(solution)/shard_map/all_to_all | solution.py:77
  20.1 101.1 %all-reduce.8.cloned.1.call-start = ((), (), s32[]{:S(2)}) async-start(), calls=%async_computation.4 | async-start | bytes 3670016 | tf_op jit(solution)/shard_map/psum | solution.py:122
  20.2 21.4 %copy-start.38 = (f32[896]{0:T(1024)}, f32[896]{0:T(1024)S(1)}, u32[]{:S(2)}) copy-start(f32[896]{0:T(1024)S(1)} %convert_element_type.242) | copy-start | bytes 10756
  20.8 17.7 %copy-start.48 = (f32[32]{0:T(128)}, f32[32]{0:T(128)S(1)}, u32[]{:S(2)}) copy-start(f32[32]{0:T(128)S(1)} %multiply_power_fusion) | copy-start | bytes 388
  21.5 114.7 %copy-start.50 = (pred[512]{0:T(512)(128)(4,1)}, pred[512]{0:T(512)(128)(4,1)S(1)}, u32[]{:S(2)}) copy-start(pred[512]{0:T(512)(128)(4,1)S(1)} %iota_compare_fusion.1) | copy-start | bytes 1540
  21.5 17.0 %copy-start.42 = (f32[512]{0:T(512)}, f32[512]{0:T(512)S(1)}, u32[]{:S(2)}) copy-start(f32[512]{0:T(512)S(1)} %iota_convert_fusion) | copy-start | bytes 6148
  21.8 16.7 %copy-start.16 = (f32[512,32]{0,1:T(8,128)}, f32[512,32]{0,1:T(8,128)S(1)}, u32[]{:S(2)}) copy-start(f32[512,32]{0,1:T(8,128)S(1)} %get-tuple-element.58) | copy-start | bytes 196612
  36.9 4.7 copy-start.44
  37.7 2.3 copy-start.22
  37.7 2.3 copy-start.24
  40.0 2.9 copy-start.2
  40.0 2.9 copy-start.34
  41.6 3.6 copy-start.36
  42.9 3.1 copy-start.6
  45.2 2.7 copy-start.11
  47.9 7.4 copy-start.54
  49.6 86.6 %all-to-all-start.2 = ((bf16[64,8,896]{2,1,0:T(8,128)(2,1)}), bf16[64,8,896]{2,1,0:T(8,128)(2,1)}, u32[]{:S(2)}, u32[]{:S(2)}) async-start(bf16[64,8,896]{2,1,0:T(8,128)(2,1)} %gather_fusion.2), calls=%async_computation.2 | async-start | bytes 1835008 | tf_op jit(solution)/shard_map/all_to_all | solution.py:78
  55.0 143.9 %all-reduce.10.cloned.1.call-start = ((), (), s32[]{:S(2)}) async-start(), calls=%async_computation.5 | async-start | bytes 1835008 | tf_op jit(solution)/shard_map/psum | solution.py:131
  55.3 69.1 %copy-start.32 = (f32[896]{0:T(1024)}, f32[896]{0:T(1024)S(1)}, u32[]{:S(2)}) copy-start(f32[896]{0:T(1024)S(1)} %convert_element_type.255) | copy-start | bytes 10756
  123.0 143.2 %copy-start.3 = (f32[512,896]{1,0:T(8,128)}, f32[512,896]{1,0:T(8,128)S(1)}, u32[]{:S(2)}) copy-start(f32[512,896]{1,0:T(8,128)S(1)} %get-tuple-element.40) | copy-start | bytes 5505028
  124.2 7.5 slice-start.5
  124.4 7.2 copy-start.12
  124.5 7.2 slice-start.6
  154.1 112.1 %all-reduce.12.cloned.1.call-start = ((), (), s32[]{:S(2)}) async-start(), calls=%async_computation.6 | async-start | bytes 3670016 | tf_op jit(solution)/shard_map/psum | solution.py:152
  154.1 6.0 copy-start.63
  166.5 174.5 %all-reduce.14.cloned.1.call-start = ((), (), s32[]{:S(2)}) async-start(), calls=%async_computation.7 | async-start | bytes 1835008 | tf_op jit(solution)/shard_map/psum | solution.py:195
  167.7 8.3 copy-start.13
  167.7 8.3 copy-start.64
  175.9 6.1 copy-start.51
  175.9 6.1 copy-start.62
  266.1 5.6 copy-start.5
  266.1 5.6 copy-start.33
  266.1 5.6 copy-start.41
  266.1 5.6 copy-start.47
  266.1 5.6 copy-start.52
  266.2 8.8 slice-start
  271.7 2.5 copy-start.7
  271.8 3.2 slice-start.1
  277.6 2.4 copy-start.23
  277.6 2.4 copy-start.25
  282.0 2.3 copy-start.17
  288.4 703.6 %all-reduce.16.cloned.1.call-start = ((), (), s32[]{:S(2)}) async-start(), calls=%async_computation.8 | async-start | bytes 59637760 | tf_op jit(solution)/shard_map/psum | solution.py:224
  289.8 3.0 copy-start.9
  307.2 11.3 %copy-start.45 = (f32[512]{0:T(512)S(1)}, f32[512]{0:T(512)}, u32[]{:S(2)}) copy-start(f32[512]{0:T(512)} %copy-done.44) | copy-start | bytes 6148
  310.1 43.6 %all-to-all-start.1 = ((bf16[64,2,3584]{2,1,0:T(2,128)(2,1)}), bf16[64,2,3584]{2,1,0:T(2,128)(2,1)}, u32[]{:S(2)}, u32[]{:S(2)}) async-start(bf16[64,2,3584]{2,1,0:T(2,128)(2,1)} %reshape.436), calls=%async_computation.1 | async-start | bytes 1835008 | tf_op jit(solution)/shard_map/all_to_all | solution.py:243
  352.4 9.6 copy-start.59
  352.4 10.3 %copy-start.60 = (s32[64]{0:T(128)S(1)}, s32[64]{0:T(128)}, u32[]{:S(2)}) copy-start(s32[64]{0:T(128)} %param.19) | copy-start | bytes 772
  353.7 304.6 %all-to-all-start.3 = ((bf16[64,2,3584]{2,1,0:T(2,128)(2,1)}), bf16[64,2,3584]{2,1,0:T(2,128)(2,1)S(1)}, u32[]{:S(2)}, u32[]{:S(2)}) async-start(bf16[64,2,3584]{2,1,0:T(2,128)(2,1)} %reshape.438), calls=%async_computation.3 | async-start | bytes 1835008 | tf_op jit(solution)/shard_map/all_to_all | solution.py:246
  373.0 3.8 copy-start.46
  992.0 2.8 copy-start.21
  992.0 3.5 copy-start.20
  992.0 4.2 copy-start.10
  997.4 8.6 copy-start.4
  997.4 13.0 %slice-start.2 = ((s8[8716288]{0:T(1024)(128)(4,1)}), s8[4194304]{0:T(1024)(128)(4,1)S(1)}, s32[]{:S(2)}) async-start(s8[8716288]{0:T(1024)(128)(4,1)} %bitcast.213), calls=%async_computation.11 | async-start | bytes 8388608
  997.4 14.6 %slice-start.3 = ((s8[8716288]{0:T(1024)(128)(4,1)}), s8[4194304]{0:T(1024)(128)(4,1)S(1)}, s32[]{:S(2)}) async-start(s8[8716288]{0:T(1024)(128)(4,1)} %bitcast.213), calls=%async_computation.12 | async-start | bytes 8388608
  1006.0 6.1 slice-start.4
  1012.1 3.5 copy-start.1
  (17 other events, 24.8 us)
Sparse Core Ops, SparseCore 0:
  48.1 73.0 all-reduce.7
  154.2 44.6 all-reduce.9
  201.4 64.7 all-reduce.11
  288.6 52.3 all-reduce.13
  345.0 646.9 all-reduce.15
where the time goes:
time: 1030 us; the launch traced here: 1020 us
  waiting for transfers between devices  511 us (50%)
  blocking collectives  281 us (27%)
  matrix products  85.3 us (8%)
  local copies, waits for them, and re-layouts  54.4 us (5%)
  other arithmetic  42 us (4%)
  starting transfers between devices  33.3 us (3%)
  between operations  16 us (2%)
    psum x1, waiting for transfers between devices, on_device(): lax.psum((statistics, grad_gain_attn, grad_w_query, grad_b_query, grad_w_...  331 us
    psum x1, blocking collectives, on_device(): lax.psum((statistics, grad_gain_attn, grad_w_query, grad_b_query, grad_w_...  281 us
    psum x1, waiting for transfers between devices, on_device(): lax.psum(dot_right(grad_gate, w_gate) + dot_right(grad_up, w_up), 'tensor')  67.2 us
    psum x1, waiting for transfers between devices, on_device(): lax.psum(jnp.dot(mixed, w_out, preferred_element_type=jnp.float32), 'tens...  65.8 us
    unnamed x158, local copies, waits for them, and re-layouts  40.9 us
    dot_general x7, matrix products, dot_left(): lax.dot_general(matrix, other, (((0,), (0,)), ((), ())), preferred_elemen...  27.9 us
    dot_general x7, matrix products, dot_right(): lax.dot_general(matrix, other, (((1,), (1,)), ((), ())), preferred_elemen...  25.9 us
    psum x1, waiting for transfers between devices, on_device(): lax.psum((dot_right(grad_q_lin, w_query) + dot_right(grad_k_lin, w_key) +...  22.4 us
  transfers between devices with their start and end apart: 9, of which 6 were waited for; matrix products, arithmetic and copies ran while one was open for 10% of the time, Pallas kernels for 0%

commit v1 on v0

--- a/solution.py
+++ b/solution.py
@@ -149,7 +149,9 @@
     grad_up = (grad_hidden * silu_gate).astype(jnp.bfloat16)
     grad_w_gate = dot_left(normed_two, grad_gate)
     grad_w_up = dot_left(normed_two, grad_up)
-    grad_normed_two = lax.psum(dot_right(grad_gate, w_gate) + dot_right(grad_up, w_up), "tensor")
+    grad_normed_two = jnp.sum(
+        lax.all_gather(dot_right(grad_gate, w_gate) + dot_right(grad_up, w_up), "tensor"), axis=0
+    )
     grad_gain_mlp = jnp.sum(grad_normed_two * residual * inverse_two, axis=0)
     scaled_two = grad_normed_two * gain_two
     grad_resid = (

time: 1030 us -> 1030 us (level)
    psum x1 -> x0, waiting for transfers between devices: 67.2 us -> none  [on_device(): lax.psum(dot_right(grad_gate, w_gate) + dot_right(grad_up, w_up), 'tensor')]
    psum x1, waiting for transfers between devices: 9.31 us -> 44.1 us  [on_device(): lax.psum(jnp.dot(hidden, w_down, preferred_element_type=jnp.float32).asty...]
    all_gather x0 -> x1, waiting for transfers between devices: none -> 22.6 us  [on_device(): lax.all_gather(dot_right(grad_gate, w_gate) + dot_right(grad_up, w_up), '...]
    unnamed x158 -> x156, local copies, waits for them, and re-layouts: 40.9 us -> 39.4 us
where the time goes in v1:
time: 1030 us; the launch traced here: 1020 us
  waiting for transfers between devices  501 us (49%)
  blocking collectives  281 us (27%)
  matrix products  88.5 us (9%)
  local copies, waits for them, and re-layouts  52.9 us (5%)
  other arithmetic  45.7 us (4%)
  starting transfers between devices  33.3 us (3%)
  between operations  16 us (2%)
    psum x1, waiting for transfers between devices, on_device(): lax.psum((statistics, grad_gain_attn, grad_w_query, grad_b_query, grad_w_...  331 us
    psum x1, blocking collectives, on_device(): lax.psum((statistics, grad_gain_attn, grad_w_query, grad_b_query, grad_w_...  281 us
    psum x1, waiting for transfers between devices, on_device(): lax.psum(jnp.dot(mixed, w_out, preferred_element_type=jnp.float32), 'tens...  65.8 us
    psum x1, waiting for transfers between devices, on_device(): lax.psum(jnp.dot(hidden, w_down, preferred_element_type=jnp.float32).asty...  44.1 us
    unnamed x156, local copies, waits for them, and re-layouts  39.4 us
    dot_general x7, matrix products, dot_left(): lax.dot_general(matrix, other, (((0,), (0,)), ((), ())), preferred_elemen...  30 us
    dot_general x7, matrix products, dot_right(): lax.dot_general(matrix, other, (((1,), (1,)), ((), ())), preferred_elemen...  26.4 us
    all_gather x1, waiting for transfers between devices, on_device(): lax.all_gather(dot_right(grad_gate, w_gate) + dot_right(grad_up, w_up), '...  22.6 us
  transfers between devices with their start and end apart: 9, of which 6 were waited for; matrix products, arithmetic and copies ran while one was open for 10% of the time, Pallas kernels for 0%

profile of v1, /device:TPU:0, one launch (start us, length us, event | category | flops | bytes accessed | tf_op | source)
XLA Modules:
  0.0 1018.3 jit_solution(13982820181397536826)
XLA Ops:
  8.4 1.6 gather_fusion
  10.0 10.1 all-to-all-start
  22.0 14.5 %all-to-all-done = bf16[64,8,896]{2,1,0:T(8,128)(2,1)S(1)} async-done(((bf16[64,8,896]{2,1,0:T(8,128)(2,1)}), bf16[64,8,896]{2,1,0:T(8,128)(2,1)S(1)}, u32[]{:S(2)}, u32[]{:S(2)}) %all-to-all-start) | async-done | bytes 917536 | tf_op jit(solution)/shard_map/all_to_all | solution.py:77
  37.7 0.8 convolution_add_fusion.1
  38.7 1.3 fusion.6
  40.0 1.5 fusion.4
  42.1 0.8 copy-done.2
  42.9 2.3 fusion.36
  45.2 0.7 copy-done.8
  46.0 2.0 fusion.103
  48.0 1.6 gather_fusion.2
  49.6 5.5 all-to-all-start.2
  55.3 65.8 %all-reduce.7.cloned.1.call-done = f32[512,896]{1,0:T(8,128)} async-done(((f32[512,896]{1,0:T(8,128)}), f32[512,896]{1,0:T(8,128)}) %all-reduce.7.cloned.1.call-update) | async-done | bytes 1835024 | tf_op jit(solution)/shard_map/psum | solution.py:122
  121.2 1.8 multiply_reduce_fusion.3
  124.4 7.2 fusion.104
  131.7 4.5 fusion.105
  136.1 10.0 multiply_convert_fusion
  146.2 6.9 fusion.106
  153.1 6.4 convolution_add_fusion
  160.6 8.3 fusion.108
  168.9 6.5 convolution_convert_fusion
  175.5 8.2 fusion.109
  183.8 7.5 fusion.65
  191.3 22.6 %all-gather.3.cloned.1.call-done = f32[1024,896]{1,0:T(8,128)} async-done(((f32[512,896]{1,0:T(8,128)}), f32[1024,896]{1,0:T(8,128)}) %all-gather.3.cloned.1.call-update) | async-done | bytes 3670032 | tf_op jit(solution)/shard_map/all_gather | solution.py:153
  213.9 3.8 reduce_sum.149
  217.7 44.1 %all-reduce.9.cloned.1.call-done = bf16[512,896]{1,0:T(8,128)(2,1)} async-done(((bf16[512,896]{1,0:T(8,128)(2,1)}), bf16[512,896]{1,0:T(8,128)(2,1)}) %all-reduce.9.cloned.1.call-update) | async-done | bytes 917520 | tf_op jit(solution)/shard_map/psum | solution.py:131
  261.9 5.5 select_reduce_fusion
  267.4 2.5 fusion.35
  270.9 2.4 fusion
  273.3 2.4 fusion.7
  275.7 0.7 convolution_bitcast_fusion
  276.5 1.2 convolution_bitcast_fusion.1
  277.8 2.3 convert_reduce_fusion.1
  280.4 0.8 copy-done.14
  282.7 1.4 add_convert_fusion
  284.4 1.1 fusion.61
  285.5 1.1 fusion.63
  286.7 1.9 fusion.59
  288.6 1.8 fusion.56
  290.4 3.8 copy.64
  294.8 8.1 reduce.8
  302.9 2.9 reshape.437
  305.8 8.4 all-to-all-start.1
  314.2 22.4 %all-reduce.11.cloned.1.call-done = bf16[512,896]{1,0:T(8,128)(2,1)} async-done(((bf16[512,896]{1,0:T(8,128)(2,1)}), bf16[512,896]{1,0:T(8,128)(2,1)}) %all-reduce.11.cloned.1.call-update) | async-done | bytes 917520 | tf_op jit(solution)/shard_map/psum | solution.py:197
  336.7 2.0 fusion.29
  338.7 1.7 fusion.55
  340.4 1.4 copy.63
  341.8 6.2 reduce.9
  348.1 1.3 reshape.439
  349.4 8.3 all-to-all-start.3
  358.4 2.0 sort.17
  361.3 2.0 pad_maximum_fusion.3
  363.3 5.4 reshape.438
  368.7 1.0 copy.62
  369.7 2.8 gather_fusion.1
  372.5 280.9 %all-reduce = (f32[896]{0:T(1024)}, f32[448]{0:T(512)}, f32[64]{0:T(128)}, f32[64]{0:T(128)}, f32[896]{0:T(1024)}, /*index=5*/f32[3]{0:T(128)S(1)}) all-reduce(f32[896]{0:T(1024)S(1)} %get-tuple-element.20, f32[448]{0:T(512)S(1)} %reduce_sum.155, f32[64]{0:T(128)S(1)} %convert_reduce_fusion.2, ...), channel_id=1, replica_groups=mesh['dp'=64,'tensor'=2] {'dp'}, use_global_device_ids=true, to_apply=%region_13.14 | all-reduce | flops 2371 | bytes 18968 | tf_op jit(solution)/shard_map/psum | solution.py:226
  654.8 1.6 gather_fusion.3
  656.4 331.3 %all-reduce.13.cloned.1.call-done = (f32[896,448]{0,1:T(8,128)}, f32[896,64]{0,1:T(8,128)}, f32[896,64]{0,1:T(8,128)}, f32[448,896]{1,0:T(8,128)}, f32[896,2432]...) async-done(((f32[896,448]{0,1:T(8,128)}, f32[896,64]{0,1:T(8,128)}, f32[896,64]{0,1:T(8,128)}, f32[448,896]{1,0:T(8,128)}, f32[896,2432]{1,0:T(8,128)}, ...) | async-done | bytes 29818896 | tf_op jit(solution)/shard_map/psum | solution.py:226
  987.7 2.8 copy.75
  991.9 1.2 copy.78
  993.1 8.6 copy.79
  1001.7 4.4 copy.80
  1006.1 1.6 slice-done.3
  1007.8 3.5 copy.81
  (198 shorter events, 15.1 us)
Async XLA Ops:
  7.2 12.9 %copy-start.55 = (bf16[64]{0:T(256)(128)(2,1)S(1)}, bf16[64]{0:T(256)(128)(2,1)}, u32[]{:S(2)}) copy-start(bf16[64]{0:T(256)(128)(2,1)} %param.26) | copy-start | bytes 388
  7.2 12.9 %copy-start.52 = (bf16[896]{0:T(1024)(128)(2,1)S(1)}, bf16[896]{0:T(1024)(128)(2,1)}, u32[]{:S(2)}) copy-start(bf16[896]{0:T(1024)(128)(2,1)} %param.20) | copy-start | bytes 5380
  7.2 13.0 %copy-start.54 = (bf16[448]{0:T(512)(128)(2,1)S(1)}, bf16[448]{0:T(512)(128)(2,1)}, u32[]{:S(2)}) copy-start(bf16[448]{0:T(512)(128)(2,1)} %param.22) | copy-start | bytes 2692
  7.2 13.0 %copy-start.56 = (bf16[64]{0:T(256)(128)(2,1)S(1)}, bf16[64]{0:T(256)(128)(2,1)}, u32[]{:S(2)}) copy-start(bf16[64]{0:T(256)(128)(2,1)} %param.24) | copy-start | bytes 388
  7.2 13.0 %copy-start.57 = (s32[64]{0:T(128)S(1)}, s32[64]{0:T(128)}, u32[]{:S(2)}) copy-start(s32[64]{0:T(128)} %param.18) | copy-start | bytes 772
  8.4 28.5 %copy-start.25 = (bf16[896,64]{0,1:T(8,128)(2,1)S(1)}, bf16[896,64]{0,1:T(8,128)(2,1)}, u32[]{:S(2)}) copy-start(bf16[896,64]{0,1:T(8,128)(2,1)} %param.23) | copy-start | bytes 344068
  10.0 27.7 %copy-start.13 = (bf16[896,448]{0,1:T(8,128)(2,1)S(1)}, bf16[896,448]{0,1:T(8,128)(2,1)}, u32[]{:S(2)}) copy-start(bf16[896,448]{0,1:T(8,128)(2,1)} %param.21) | copy-start | bytes 2408452
  10.0 26.5 %all-to-all-start = ((bf16[64,8,896]{2,1,0:T(8,128)(2,1)}), bf16[64,8,896]{2,1,0:T(8,128)(2,1)S(1)}, u32[]{:S(2)}, u32[]{:S(2)}) async-start(bf16[64,8,896]{2,1,0:T(8,128)(2,1)} %gather_fusion), calls=%async_computation | async-start | bytes 1835008 | tf_op jit(solution)/shard_map/all_to_all | solution.py:77
  20.1 101.1 %all-reduce.7.cloned.1.call-start = ((), (), s32[]{:S(2)}) async-start(), calls=%async_computation.4 | async-start | bytes 3670016 | tf_op jit(solution)/shard_map/psum | solution.py:122
  20.2 21.4 %copy-start.37 = (f32[896]{0:T(1024)}, f32[896]{0:T(1024)S(1)}, u32[]{:S(2)}) copy-start(f32[896]{0:T(1024)S(1)} %convert_element_type.242) | copy-start | bytes 10756
  20.8 17.7 %copy-start.47 = (f32[32]{0:T(128)}, f32[32]{0:T(128)S(1)}, u32[]{:S(2)}) copy-start(f32[32]{0:T(128)S(1)} %multiply_power_fusion) | copy-start | bytes 388
  21.5 114.7 %copy-start.49 = (pred[512]{0:T(512)(128)(4,1)}, pred[512]{0:T(512)(128)(4,1)S(1)}, u32[]{:S(2)}) copy-start(pred[512]{0:T(512)(128)(4,1)S(1)} %iota_compare_fusion.1) | copy-start | bytes 1540
  21.5 17.0 %copy-start.41 = (f32[512]{0:T(512)}, f32[512]{0:T(512)S(1)}, u32[]{:S(2)}) copy-start(f32[512]{0:T(512)S(1)} %iota_convert_fusion) | copy-start | bytes 6148
  21.8 16.7 %copy-start.15 = (f32[512,32]{0,1:T(8,128)}, f32[512,32]{0,1:T(8,128)S(1)}, u32[]{:S(2)}) copy-start(f32[512,32]{0,1:T(8,128)S(1)} %get-tuple-element.58) | copy-start | bytes 196612
  36.9 4.7 copy-start.43
  37.7 2.3 copy-start.21
  37.7 2.3 copy-start.23
  40.0 2.9 copy-start.2
  40.0 2.9 copy-start.33
  41.6 3.6 copy-start.35
  42.9 3.1 copy-start.6
  45.2 2.7 copy-start.11
  47.9 7.4 copy-start.53
  49.6 86.6 %all-to-all-start.2 = ((bf16[64,8,896]{2,1,0:T(8,128)(2,1)}), bf16[64,8,896]{2,1,0:T(8,128)(2,1)}, u32[]{:S(2)}, u32[]{:S(2)}) async-start(bf16[64,8,896]{2,1,0:T(8,128)(2,1)} %gather_fusion.2), calls=%async_computation.2 | async-start | bytes 1835008 | tf_op jit(solution)/shard_map/all_to_all | solution.py:78
  55.0 158.9 %all-gather.3.cloned.1.call-start = ((), (), s32[]{:S(2)}) async-start(), calls=%async_computation.7 | async-start | bytes 5505024 | tf_op jit(solution)/shard_map/all_gather | solution.py:153
  55.3 69.1 %copy-start.31 = (f32[896]{0:T(1024)}, f32[896]{0:T(1024)S(1)}, u32[]{:S(2)}) copy-start(f32[896]{0:T(1024)S(1)} %convert_element_type.255) | copy-start | bytes 10756
  123.0 138.9 %copy-start.3 = (f32[512,896]{1,0:T(8,128)}, f32[512,896]{1,0:T(8,128)S(1)}, u32[]{:S(2)}) copy-start(f32[512,896]{1,0:T(8,128)S(1)} %get-tuple-element.40) | copy-start | bytes 5505028
  124.2 7.5 slice-start.5
  124.4 7.2 copy-start.12
  124.4 7.2 slice-start.6
  146.1 6.9 copy-start.63
  146.1 6.9 copy-start.62
  159.4 102.4 %all-reduce.9.cloned.1.call-start = ((), (), s32[]{:S(2)}) async-start(), calls=%async_computation.5 | async-start | bytes 1835008 | tf_op jit(solution)/shard_map/psum | solution.py:131
  160.6 8.3 copy-start.60
  175.5 161.2 %all-reduce.11.cloned.1.call-start = ((), (), s32[]{:S(2)}) async-start(), calls=%async_computation.6 | async-start | bytes 1835008 | tf_op jit(solution)/shard_map/psum | solution.py:197
  175.5 8.2 copy-start.50
  175.5 8.2 copy-start.61
  261.8 5.6 copy-start.4
  261.8 5.6 copy-start.32
  261.8 5.6 copy-start.40
  261.8 5.6 copy-start.46
  261.9 5.6 copy-start.51
  261.9 8.8 slice-start
  267.4 2.5 copy-start.7
  267.4 3.2 slice-start.1
  273.3 2.4 copy-start.22
  273.3 2.4 copy-start.24
  277.7 2.3 copy-start.16
  284.1 703.6 %all-reduce.13.cloned.1.call-start = ((), (), s32[]{:S(2)}) async-start(), calls=%async_computation.8 | async-start | bytes 59637760 | tf_op jit(solution)/shard_map/psum | solution.py:226
  285.5 3.0 copy-start.9
  302.9 11.3 %copy-start.44 = (f32[512]{0:T(512)S(1)}, f32[512]{0:T(512)}, u32[]{:S(2)}) copy-start(f32[512]{0:T(512)} %copy-done.43) | copy-start | bytes 6148
  305.8 43.6 %all-to-all-start.1 = ((bf16[64,2,3584]{2,1,0:T(2,128)(2,1)}), bf16[64,2,3584]{2,1,0:T(2,128)(2,1)}, u32[]{:S(2)}, u32[]{:S(2)}) async-start(bf16[64,2,3584]{2,1,0:T(2,128)(2,1)} %reshape.437), calls=%async_computation.1 | async-start | bytes 1835008 | tf_op jit(solution)/shard_map/all_to_all | solution.py:245
  348.1 9.6 copy-start.58
  348.1 10.3 %copy-start.59 = (s32[64]{0:T(128)S(1)}, s32[64]{0:T(128)}, u32[]{:S(2)}) copy-start(s32[64]{0:T(128)} %param.19) | copy-start | bytes 772
  349.4 304.6 %all-to-all-start.3 = ((bf16[64,2,3584]{2,1,0:T(2,128)(2,1)}), bf16[64,2,3584]{2,1,0:T(2,128)(2,1)S(1)}, u32[]{:S(2)}, u32[]{:S(2)}) async-start(bf16[64,2,3584]{2,1,0:T(2,128)(2,1)} %reshape.439), calls=%async_computation.3 | async-start | bytes 1835008 | tf_op jit(solution)/shard_map/all_to_all | solution.py:248
  368.7 3.8 copy-start.45
  987.7 2.8 copy-start.20
  987.7 3.5 copy-start.19
  987.7 4.2 copy-start.10
  993.1 8.6 copy-start.5
  993.1 13.0 %slice-start.2 = ((s8[8716288]{0:T(1024)(128)(4,1)}), s8[4194304]{0:T(1024)(128)(4,1)S(1)}, s32[]{:S(2)}) async-start(s8[8716288]{0:T(1024)(128)(4,1)} %bitcast.214), calls=%async_computation.11 | async-start | bytes 8388608
  993.1 14.6 %slice-start.3 = ((s8[8716288]{0:T(1024)(128)(4,1)}), s8[4194304]{0:T(1024)(128)(4,1)S(1)}, s32[]{:S(2)}) async-start(s8[8716288]{0:T(1024)(128)(4,1)} %bitcast.214), calls=%async_computation.12 | async-start | bytes 8388608
  1001.7 6.1 slice-start.4
  1007.8 3.5 copy-start.1
  (16 other events, 23.3 us)
Sparse Core Ops, SparseCore 0:
  48.1 73.0 all-reduce.6
  159.6 54.3 all-gather.2
  217.1 44.6 all-reduce.8
  284.2 52.3 all-reduce.10
  341.1 646.6 all-reduce.12
